TPU v7x, 32 devices: a whole 2x2x4 slice. The times are simulated.
32 devices in a mesh: req: 4 (over z), mlp: 8 (over y, x, core).
Axes of the slice: x: 2, y: 2, z: 4, core: 2. Of those that a mesh axis runs over, the one named last changes fastest.
Arguments:
- tokens: bfloat16 [1024, 5120], P(('req', 'mlp')), may hold values from -6 to 6
- modulation: float32 [16, 6, 5120], P('req'), may hold values from -3 to 3
- lengths: int32 [4, 4], P('req'), may hold values from 1 to 160, 256 in all within a row
- request_adapter: int32 [16], P('req'), may hold values from 0 to 31
- adapter_storage: int32 [32], replicated, may hold values from 0 to 31, each once
- adapter_down_weight: bfloat16 [32, 5120, 32], P('mlp'), may hold values from -0.078125 to 0.078125
- adapter_up_maps: bfloat16 [32, 2, 16, 4096], P('mlp'), may hold values from -1.5 to 1.5
- input_projection: bfloat16 [4, 5120, 4096], P(None, None, 'mlp'), may hold values from -0.078125 to 0.078125
- query_key_gains: float32 [3, 4096], P(None, 'mlp'), may hold values from 0.1 to 1.9
- positions: int32 [3, 1024], P(None, 'req'), may hold values from 0 to 63
- block_page_lookup: int32 [4, 16], P('req'), may hold values from 0 to 15, each once within a row
- output_projection: bfloat16 [2, 4096, 5120], P(None, 'mlp'), may hold values from -0.09375 to 0.09375
- cross_norm_gain: float32 [5120], replicated, may hold values from 0.1 to 1.9
- text_token_cache: bfloat16 [2, 16, 512, 4096], P(None, 'req', None, 'mlp'), may hold values from -3 to 3
- feedforward_up: bfloat16 [5120, 8192], P('req', 'mlp'), may hold values from -0.078125 to 0.078125
- feedforward_down: bfloat16 [8192, 5120], P('mlp', 'req'), may hold values from -0.0625 to 0.0625
Outputs:
- layer_out: bfloat16 [1024, 5120], P(('req', 'mlp'))
- kv_pages: bfloat16 [2, 64, 16, 4096], P(None, 'req', None, 'mlp')
Inputs may be any that keep to these rules, and one draw needn't show every extreme that they name: `lengths`: row g lists the token counts of the 4 requests of group g in order; they fill the group's 256 positions, and the largest is 160. A permutation: adapter a is stored at index adapter_storage[a] of adapter_down_weight and adapter_up_maps. `block_page_lookup`: each row is a permutation of a group's 16 pages.
All inputs are finite; a program needn't handle non-finite values.
Results may differ from a plain program's by a relative error of at most 0.017.
Values may be sent and summed in bfloat16 or wider, within the bound.
A program may use at most 192 MiB of HBM per device.

v0:
```python
import math
import jax
import jax.numpy as jnp
from jax import lax
from jax.sharding import PartitionSpec as P

HD = 128
PAGE = 16
EPSILON = 1e-06


def as_sent(array):

    def short(part):
        return part.astype(jnp.bfloat16) if part.dtype == jnp.float32 else part

    return jax.tree.map(short, array)


def layer_norm(values):
    center = values - jnp.mean(values, axis=-1, keepdims=True)
    spread = jnp.mean(center * center, axis=-1, keepdims=True)
    return center * lax.rsqrt(spread + EPSILON)


def rotary_tables(grid):
    half_dim = HD // 2
    spatial = half_dim // 3
    temporal = half_dim - 2 * spatial
    column = jnp.arange(half_dim, dtype=jnp.int32)
    which_axis = jnp.where(
        column < temporal, 0, jnp.where(column < temporal + spatial, 1, 2)
    ).astype(jnp.int32)
    offset = jnp.where(
        which_axis == 0, 0, jnp.where(which_axis == 1, temporal, temporal + spatial)
    ).astype(jnp.int32)
    span_size = jnp.where(which_axis == 0, temporal, spatial).astype(jnp.float32)
    frequency = jnp.exp(-(column - offset).astype(jnp.float32) / span_size * math.log(10000.0))
    coordinate = grid.astype(jnp.float32)[which_axis, :].T
    angles = coordinate * frequency[None, :]
    return (jnp.cos(angles), jnp.sin(angles))


def rotate(values, cosine, sine_part):
    half_dim = HD // 2
    front_half = values[..., :half_dim]
    back_half = values[..., half_dim:]
    cosine = cosine[:, None, :]
    sine_part = sine_part[:, None, :]
    return jnp.concatenate(
        [front_half * cosine - back_half * sine_part, back_half * cosine + front_half * sine_part],
        axis=-1,
    )


def attend(queries, key_rows, value_rows, allowed):
    scores = jnp.einsum(
        "thd,shd->hts", queries, key_rows, preferred_element_type=jnp.float32
    ) / math.sqrt(HD)
    scores = jnp.where(allowed[None], scores, -1e30)
    weights = jnp.exp(scores)
    weights = (weights / jnp.sum(weights, axis=-1, keepdims=True)).astype(jnp.bfloat16)
    return jnp.einsum(
        "hts,shd->thd", weights, value_rows, preferred_element_type=jnp.float32
    ).astype(jnp.bfloat16)


def choose_rows(table, segment):
    chosen = jnp.zeros((segment.shape[0],) + table.shape[1:], table.dtype)
    for request in range(table.shape[0]):
        picked = (segment == request).reshape((-1,) + (1,) * (table.ndim - 1))
        chosen = jnp.where(picked, table[request][None], chosen)
    return chosen


def body(
    tokens,
    modulation,
    lengths,
    request_adapter,
    adapter_storage,
    adapter_down_weight,
    adapter_up_maps,
    input_projection,
    query_key_gains,
    positions,
    block_page_lookup,
    output_projection,
    cross_norm_gain,
    text_token_cache,
    feedforward_up,
    feedforward_down,
):
    mlp_count = lax.axis_size("mlp")
    my_index = lax.axis_index("mlp")
    own_count = tokens.shape[0]
    group_rows = own_count * mlp_count
    local_width = input_projection.shape[2]
    heads_local = local_width // HD
    entire_width = local_width * mlp_count
    resident_slots = adapter_down_weight.shape[0]
    doubled_rank = adapter_down_weight.shape[2]
    rank_once = doubled_rank // 2

    def over_group(own_rows, row_fn):
        return row_fn(lax.all_gather(own_rows, "mlp", axis=0, tiled=True), jnp.int32(0))

    def sum_rows(term_fn):
        return lax.psum_scatter(
            term_fn(jnp.int32(0), own_count * lax.axis_size("mlp")).astype(jnp.bfloat16),
            "mlp",
            scatter_dimension=0,
            tiled=True,
        ).astype(jnp.float32)

    def global_sum(pieces):
        return jax.tree.map(lambda part: part.astype(jnp.float32), lax.psum(as_sent(pieces), "mlp"))

    up_full, down_full = (
        lax.all_gather(feedforward_up, "req", axis=0, tiled=True),
        lax.all_gather(feedforward_down, "req", axis=1, tiled=True),
    )
    adapter_up_weight = lax.all_to_all(
        adapter_up_maps, "mlp", split_axis=3, concat_axis=0, tiled=True
    )
    slot_total = adapter_up_weight.shape[0]
    bounds = jnp.cumsum(lengths[0])
    position = jnp.arange(group_rows, dtype=jnp.int32)
    segment = jnp.sum((position[:, None] >= bounds[None, :]).astype(jnp.int32), axis=1)
    own_start = my_index * own_count
    own_segment = lax.dynamic_slice_in_dim(segment, own_start, own_count)
    per_token = [choose_rows(modulation[:, which_row, :], own_segment) for which_row in range(6)]
    token_f32 = tokens.astype(jnp.float32)
    normed_in = (layer_norm(token_f32) * (1.0 + per_token[1]) + per_token[0]).astype(jnp.bfloat16)

    def project_rows(incoming_rows, row_start):
        row_total = incoming_rows.shape[0]
        parts = [
            jnp.dot(incoming_rows, input_projection[which_map], preferred_element_type=jnp.float32)
            for which_map in range(3)
        ]
        code_block = jnp.einsum(
            "lf,sfe->lse", incoming_rows, adapter_down_weight, preferred_element_type=jnp.float32
        )
        parts.append(code_block.reshape(row_total, resident_slots * doubled_rank))
        return jnp.concatenate(parts, axis=1)

    projected = over_group(normed_in, project_rows)
    query_base = projected[:, :local_width]
    key_linear = projected[:, local_width : 2 * local_width]
    value_base = projected[:, 2 * local_width : 3 * local_width]
    code_block = projected[:, 3 * local_width :].reshape(group_rows, resident_slots, doubled_rank)
    request_slot = adapter_storage[request_adapter]
    token_slot = choose_rows(request_slot, segment)
    held = (
        token_slot[:, None]
        == my_index * resident_slots + jnp.arange(resident_slots, dtype=jnp.int32)[None, :]
    ).astype(jnp.float32)
    my_codes = jnp.sum(held[:, :, None] * code_block, axis=1)
    codes = global_sum(my_codes).astype(jnp.bfloat16)
    everywhere = (token_slot[:, None] == jnp.arange(slot_total, dtype=jnp.int32)[None, :]).astype(
        jnp.float32
    )

    def spread(code_part):
        return (
            (everywhere[:, :, None] * code_part[:, None, :].astype(jnp.float32))
            .reshape(group_rows, slot_total * rank_once)
            .astype(jnp.bfloat16)
        )

    query_up_weight = adapter_up_weight[:, 0].reshape(slot_total * rank_once, local_width)
    value_up_weight = adapter_up_weight[:, 1].reshape(slot_total * rank_once, local_width)
    query_linear = query_base + jnp.dot(
        spread(codes[:, :rank_once]), query_up_weight, preferred_element_type=jnp.float32
    )
    value_rows = (
        value_base
        + jnp.dot(spread(codes[:, rank_once:]), value_up_weight, preferred_element_type=jnp.float32)
    ).astype(jnp.bfloat16)
    query_square, key_square = global_sum(
        (jnp.sum(query_linear * query_linear, axis=1), jnp.sum(key_linear * key_linear, axis=1))
    )
    query_norm = (
        query_linear
        * lax.rsqrt(query_square / entire_width + EPSILON)[:, None]
        * query_key_gains[0]
    )
    key_norm = (
        key_linear * lax.rsqrt(key_square / entire_width + EPSILON)[:, None] * query_key_gains[1]
    )
    cosine, sine_part = rotary_tables(positions)
    query_rot = rotate(query_norm.reshape(group_rows, heads_local, HD), cosine, sine_part).astype(
        jnp.bfloat16
    )
    key_rot = rotate(key_norm.reshape(group_rows, heads_local, HD), cosine, sine_part).astype(
        jnp.bfloat16
    )
    value_heads = value_rows.reshape(group_rows, heads_local, HD)
    page_count = group_rows // PAGE
    stacked = jnp.stack(
        [
            key_rot.reshape(page_count, PAGE, local_width),
            value_rows.reshape(page_count, PAGE, local_width),
        ]
    )
    kv_pages = jnp.zeros_like(stacked).at[:, block_page_lookup[0]].set(stacked)
    allowed = segment[:, None] == segment[None, :]
    attended = attend(query_rot, key_rot, value_heads, allowed).reshape(group_rows, local_width)
    text_owner = (
        jnp.arange(text_token_cache.shape[1] * text_token_cache.shape[2], dtype=jnp.int32)
        // text_token_cache.shape[2]
    )
    cross_allowed = segment[:, None] == text_owner[None, :]
    text_keys = text_token_cache[0].reshape(-1, heads_local, HD)
    text_values = text_token_cache[1].reshape(-1, heads_local, HD)

    def attend_term(row_start, row_total):
        return jnp.dot(attended, output_projection[0], preferred_element_type=jnp.float32)

    first_res = (token_f32 + per_token[2] * sum_rows(attend_term)).astype(jnp.bfloat16)
    cross_own = (layer_norm(first_res.astype(jnp.float32)) * cross_norm_gain).astype(jnp.bfloat16)

    def cross_rows(incoming_rows, row_start):
        return jnp.dot(incoming_rows, input_projection[3], preferred_element_type=jnp.float32)

    cross_linear = over_group(cross_own, cross_rows)
    cross_square = global_sum(jnp.sum(cross_linear * cross_linear, axis=1))
    cross_query = (
        cross_linear
        * lax.rsqrt(cross_square / entire_width + EPSILON)[:, None]
        * query_key_gains[2]
    ).astype(jnp.bfloat16)
    cross_out = attend(
        cross_query.reshape(group_rows, heads_local, HD), text_keys, text_values, cross_allowed
    ).reshape(group_rows, local_width)

    def cross_term(row_start, row_total):
        return jnp.dot(cross_out, output_projection[1], preferred_element_type=jnp.float32)

    second_res = (first_res.astype(jnp.float32) + sum_rows(cross_term)).astype(jnp.bfloat16)
    mlp_own = (
        layer_norm(second_res.astype(jnp.float32)) * (1.0 + per_token[4]) + per_token[3]
    ).astype(jnp.bfloat16)

    def expand_rows(incoming_rows, row_start):
        return jax.nn.gelu(
            jnp.dot(incoming_rows, up_full, preferred_element_type=jnp.float32), approximate=True
        ).astype(jnp.bfloat16)

    hidden = over_group(mlp_own, expand_rows)

    def down_term(row_start, row_total):
        return jnp.dot(hidden, down_full, preferred_element_type=jnp.float32)

    layer_out = (second_res.astype(jnp.float32) + per_token[5] * sum_rows(down_term)).astype(
        jnp.bfloat16
    )
    return (layer_out, kv_pages)


def solution(mesh):
    return jax.shard_map(
        body,
        mesh=mesh,
        in_specs=(
            P(("req", "mlp"), None),
            P("req", None, None),
            P("req", None),
            P("req"),
            P(),
            P("mlp", None, None),
            P("mlp", None, None, None),
            P(None, None, "mlp"),
            P(None, "mlp"),
            P(None, "req"),
            P("req", None),
            P(None, "mlp", None),
            P(),
            P(None, "req", None, "mlp"),
            P("req", "mlp"),
            P("mlp", "req"),
        ),
        out_specs=(P(("req", "mlp"), None), P(None, "req", None, "mlp")),
        check_vma=False,
    )
```

profile of v0, /device:TPU:0, one launch (start us, length us, event | category | flops | bytes accessed | tf_op | source)
XLA Modules:
  0.0 720.8 jit_solution(13914493310342817437)
XLA Ops:
  8.1 2.6 fusion.93
  10.7 0.8 reduce-window.8
  11.7 1.1 convert_reduce_fusion.2
  12.9 1.2 fusion.48
  14.1 2.1 fusion.51
  16.2 11.0 %copy.88 = bf16[4,2,16,4096]{2,0,1,3:T(4,128)(2,1)} copy(bf16[4,2,16,4096]{3,2,1,0:T(8,128)(2,1)} %param.22) | data formatting | bytes 2097152 | tf_op args[6]
  27.2 11.3 %reshape.439 = bf16[8,2,32768]{2,1,0:T(2,128)(2,1)} reshape(bf16[4096,2,4,16]{3,2,1,0:T(4,128)(2,1)} %bitcast.123) | data formatting | bytes 2097152
  38.5 5.2 all-to-all-start
  45.1 0.7 fusion.96
  45.8 2.5 compare_select_fusion.10
  48.7 0.8 copy.94
  50.8 0.7 broadcast_compare_fusion.1
  51.5 8.3 %all-to-all-done = bf16[8,2,32768]{2,1,0:T(2,128)(2,1)S(1)} async-done(((bf16[8,2,32768]{2,1,0:T(2,128)(2,1)}), bf16[8,2,32768]{2,1,0:T(2,128)(2,1)S(1)}, u32[]{:S(2)}, u32[]{:S(2)}) %all-to-all-start) | async-done | bytes 1048608 | tf_op jit(solution)/shard_map/all_to_all | solution.py:123
  59.8 7.6 %reshape.440 = bf16[4096,2,4,16]{3,2,1,0:T(4,128)(2,1)} reshape(bf16[8,2,32768]{2,1,0:T(2,128)(2,1)S(1)} %all-to-all-done) | data formatting | bytes 2097152
  67.3 10.8 %copy.106 = bf16[4,2,16,8,512]{4,2,1,0,3:T(8,128)(2,1)S(1)} copy(bf16[4,2,16,8,512]{2,0,1,4,3:T(4,128)(2,1)} %bitcast.122) | data formatting | bytes 2097152 | tf_op jit(solution)/shard_map/all_to_all | solution.py:123
  78.2 2.7 fusion.99
  81.0 22.3 %psum.28 = bf16[256,32]{0,1:T(8,128)(2,1)S(1)} all-reduce(bf16[256,32]{0,1:T(8,128)(2,1)S(1)} %multiply_reduce_fusion.3), channel_id=1, replica_groups=mesh['req'=4,'mlp'=8] {'mlp'}, use_global_device_ids=true, to_apply=%region_5.6 | all-reduce | flops 8192 | bytes 32768 | tf_op jit(solution)/shard_map/psum | solution.py:117
  103.3 1.6 multiply_convert_fusion.1
  104.9 4.9 fusion.7
  110.3 4.1 multiply_reduce_fusion.1
  114.4 12.0 %all-reduce = (bf16[256]{0:T(256)(128)(2,1)S(1)}, bf16[256]{0:T(256)(128)(2,1)S(1)}) all-reduce(bf16[256]{0:T(256)(128)(2,1)S(1)} %get-tuple-element.62, bf16[256]{0:T(256)(128)(2,1)S(1)} %get-tuple-element.64), channel_id=1, replica_groups=mesh['req'=4,'mlp'=8] {'mlp'}, use_global_device_ids=true, to_apply=%region_9.10 | all-reduce | flops 512 | bytes 2048 | tf_op jit(solution)/shard_map/psum | solution.py:117
  127.7 4.8 fusion.9
  132.9 0.8 copy.107
  134.7 1.3 convolution_convert_fusion.3
  136.1 5.6 convolution_convert_fusion.2
  141.7 1.2 fusion.94
  142.9 42.6 %reduce-scatter.4.cloned.1.call-done = bf16[32,5120]{1,0:T(8,128)(2,1)} async-done(((bf16[256,5120]{1,0:T(8,128)(2,1)}), bf16[32,5120]{1,0:T(8,128)(2,1)}) %reduce-scatter.4.cloned.1.call-update) | async-done | bytes 327696 | tf_op jit(solution)/shard_map/reduce_scatter | solution.py:109
  185.5 1.4 convert_reduce_fusion.1
  187.1 0.9 fusion.47
  188.1 4.0 fusion.89
  192.1 4.0 reshape_squeeze.14
  196.1 2.1 reshape.438
  198.6 19.7 %all-gather.8.cloned.1.call-done = bf16[256,5120]{1,0:T(8,128)(2,1)} async-done(((bf16[32,5120]{1,0:T(8,128)(2,1)}), bf16[256,5120]{1,0:T(8,128)(2,1)}) %all-gather.8.cloned.1.call-update) | async-done | bytes 2621456 | tf_op jit(solution)/shard_map/all_gather | solution.py:106
  218.3 5.6 multiply_reduce_fusion
  223.9 13.3 %psum.31 = bf16[256]{0:T(256)(128)(2,1)S(1)} all-reduce(bf16[256]{0:T(256)(128)(2,1)S(1)} %get-tuple-element.66), channel_id=1, replica_groups=mesh['req'=4,'mlp'=8] {'mlp'}, use_global_device_ids=true, to_apply=%region_15.16 | all-reduce | flops 256 | bytes 1024 | tf_op jit(solution)/shard_map/psum | solution.py:117
  237.3 6.4 fusion
  243.6 5.9 fusion.24
  249.6 3.1 convolution_convert_fusion.1
  254.0 42.6 %reduce-scatter.6.cloned.1.call-done = bf16[32,5120]{1,0:T(8,128)(2,1)} async-done(((bf16[256,5120]{1,0:T(8,128)(2,1)}), bf16[32,5120]{1,0:T(8,128)(2,1)}) %reduce-scatter.6.cloned.1.call-update) | async-done | bytes 327696 | tf_op jit(solution)/shard_map/reduce_scatter | solution.py:109
  296.6 1.2 convert_reduce_fusion
  298.1 1.1 fusion.44
  299.6 139.0 %all-gather.12.cloned.1.call-done = bf16[5120,1024]{1,0:T(8,128)(2,1)} async-done(((bf16[1280,1024]{1,0:T(8,128)(2,1)}), bf16[5120,1024]{1,0:T(8,128)(2,1)}) %all-gather.12.cloned.1.call-update) | async-done | bytes 10485776 | tf_op jit(solution)/shard_map/all_gather | solution.py:120
  438.6 183.4 %all-gather.14.cloned.1.call-done = bf16[1024,5120]{1,0:T(8,128)(2,1)} async-done(((bf16[1024,1280]{1,0:T(8,128)(2,1)}), bf16[1024,5120]{1,0:T(8,128)(2,1)}) %all-gather.14.cloned.1.call-update) | async-done | bytes 10485776 | tf_op jit(solution)/shard_map/all_gather | solution.py:121
  622.0 30.5 %all-gather.10.cloned.1.call-done = bf16[256,5120]{1,0:T(8,128)(2,1)} async-done(((bf16[32,5120]{1,0:T(8,128)(2,1)}), bf16[256,5120]{1,0:T(8,128)(2,1)}) %all-gather.10.cloned.1.call-update) | async-done | bytes 2621456 | tf_op jit(solution)/shard_map/all_gather | solution.py:106
  652.5 15.1 %convolution_convert_fusion = bf16[256,5120]{1,0:T(8,128)(2,1)} fusion(bf16[1024,5120]{1,0:T(8,128)(2,1)} %all-gather.14.cloned.1.call-done, bf16[256,5120]{1,0:T(8,128)(2,1)} %all-gather.10.cloned.1.call-done, bf16[5120,1024]{1,0:T(8,128)(2,1)} %all-gather.12.cloned.1.call-done), kind=kOutput, calls=%fused_computation.6 | convolution fusion | flops 5372379136 | bytes 26214400 | tf_op jit(solution)/shard_map/dot_general | solution.py:254
  668.2 1.2 scatter_fusion
  669.5 42.0 %reduce-scatter.8.cloned.1.call-done = bf16[32,5120]{1,0:T(8,128)(2,1)} async-done(((bf16[256,5120]{1,0:T(8,128)(2,1)}), bf16[32,5120]{1,0:T(8,128)(2,1)}) %reduce-scatter.8.cloned.1.call-update) | async-done | bytes 327696 | tf_op jit(solution)/shard_map/reduce_scatter | solution.py:109
  711.5 2.0 fusion.54
  (150 shorter events, 9.5 us)
Async XLA Ops:
  8.0 70.2 %copy-start = (bf16[4,5120,32]{1,2,0:T(8,128)(2,1)S(1)}, bf16[4,5120,32]{1,2,0:T(8,128)(2,1)}, u32[]{:S(2)}) copy-start(bf16[4,5120,32]{1,2,0:T(8,128)(2,1)} %param.21) | copy-start | bytes 3932164
  8.0 70.2 %all-gather.6.cloned.1.call-start = ((), (), s32[]{:S(2)}) async-start(), calls=%async_computation.4 | async-start | bytes 2949120 | tf_op jit(solution)/shard_map/all_gather | solution.py:106
  11.7 15.5 %copy-start.27 = (pred[32]{0:T(512)(128)(4,1)}, pred[32]{0:T(512)(128)(4,1)S(1)}, u32[]{:S(2)}) copy-start(pred[32]{0:T(512)(128)(4,1)S(1)} %get-tuple-element.60) | copy-start | bytes 100
  11.7 15.5 %copy-start.29 = (pred[32]{0:T(512)(128)(4,1)}, pred[32]{0:T(512)(128)(4,1)S(1)}, u32[]{:S(2)}) copy-start(pred[32]{0:T(512)(128)(4,1)S(1)} %get-tuple-element.61) | copy-start | bytes 100
  27.2 16.5 %copy-start.34 = (s32[3,256]{1,0:T(4,128)S(1)}, s32[3,256]{1,0:T(4,128)}, u32[]{:S(2)}) copy-start(s32[3,256]{1,0:T(4,128)} %param.25) | copy-start | bytes 9220
  27.2 16.6 %copy-start.36 = (s32[4]{0:T(128)S(1)}, s32[4]{0:T(128)}, u32[]{:S(2)}) copy-start(s32[4]{0:T(128)} %param.19) | copy-start | bytes 52
  27.2 16.6 %copy-start.2 = (s32[32]{0:T(128)S(1)}, s32[32]{0:T(128)}, u32[]{:S(2)}) copy-start(s32[32]{0:T(128)} %param.20) | copy-start | bytes 388
  27.2 22.4 %copy-start.33 = (f32[3,512]{1,0:T(4,128)S(1)}, f32[3,512]{1,0:T(4,128)}, u32[]{:S(2)}) copy-start(f32[3,512]{1,0:T(4,128)} %param.24) | copy-start | bytes 18436
  38.5 21.3 %all-to-all-start = ((bf16[8,2,32768]{2,1,0:T(2,128)(2,1)}), bf16[8,2,32768]{2,1,0:T(2,128)(2,1)S(1)}, u32[]{:S(2)}, u32[]{:S(2)}) async-start(bf16[8,2,32768]{2,1,0:T(2,128)(2,1)} %reshape.439), calls=%async_computation | async-start | bytes 2097152 | tf_op jit(solution)/shard_map/all_to_all | solution.py:123
  43.7 141.8 %reduce-scatter.4.cloned.1.call-start = ((), (), s32[]{:S(2)}) async-start(), calls=%async_computation.5 | async-start | bytes 2949120 | tf_op jit(solution)/shard_map/reduce_scatter | solution.py:109
  104.9 5.3 copy-start.4
  110.3 16.2 %copy-start.32 = (f32[1,512]{1,0:T(1,128)S(1)}, f32[1,512]{1,0:T(1,128)}, u32[]{:S(2)}) copy-start(f32[1,512]{1,0:T(1,128)} %get-tuple-element.54) | copy-start | bytes 6148
  110.3 16.8 %copy-start.31 = (f32[1,512]{1,0:T(1,128)S(1)}, f32[1,512]{1,0:T(1,128)}, u32[]{:S(2)}) copy-start(f32[1,512]{1,0:T(1,128)} %get-tuple-element.53) | copy-start | bytes 6148
  127.7 4.9 copy-start.13
  127.7 6.1 copy-start.12
  132.9 3.1 copy-start.5
  136.0 49.5 %copy-start.3 = (bf16[32,5120]{1,0:T(8,128)(2,1)S(1)}, bf16[32,5120]{1,0:T(8,128)(2,1)}, u32[]{:S(2)}) copy-start(bf16[32,5120]{1,0:T(8,128)(2,1)} %param.16) | copy-start | bytes 983044
  136.0 49.4 %copy-start.25 = (f32[1,1,5120]{2,0,1:T(1,128)S(1)}, f32[1,1,5120]{2,0,1:T(1,128)}, u32[]{:S(2)}) copy-start(f32[1,1,5120]{2,0,1:T(1,128)} %get-tuple-element.40) | copy-start | bytes 61444
  136.0 49.4 %copy-start.28 = (pred[32]{0:T(512)(128)(4,1)S(1)}, pred[32]{0:T(512)(128)(4,1)}, u32[]{:S(2)}) copy-start(pred[32]{0:T(512)(128)(4,1)} %copy-done.27) | copy-start | bytes 100
  136.0 49.4 %copy-start.30 = (pred[32]{0:T(512)(128)(4,1)S(1)}, pred[32]{0:T(512)(128)(4,1)}, u32[]{:S(2)}) copy-start(pred[32]{0:T(512)(128)(4,1)} %copy-done.29) | copy-start | bytes 100
  136.1 51.1 %copy-start.26 = (f32[5120]{0:T(1024)S(1)}, f32[5120]{0:T(1024)}, u32[]{:S(2)}) copy-start(f32[5120]{0:T(1024)} %param.28) | copy-start | bytes 61444
  141.7 76.6 %all-gather.8.cloned.1.call-start = ((), (), s32[]{:S(2)}) async-start(), calls=%async_computation.6 | async-start | bytes 2949120 | tf_op jit(solution)/shard_map/all_gather | solution.py:106
  188.1 108.6 %reduce-scatter.6.cloned.1.call-start = ((), (), s32[]{:S(2)}) async-start(), calls=%async_computation.7 | async-start | bytes 2949120 | tf_op jit(solution)/shard_map/reduce_scatter | solution.py:109
  198.6 38.6 %copy-start.10 = (bf16[2048,4,128]{2,1,0:T(4,128)(2,1)S(1)}, bf16[2048,4,128]{2,1,0:T(4,128)(2,1)}, u32[]{:S(2)}) copy-start(bf16[2048,4,128]{2,1,0:T(4,128)(2,1)} %reshape_squeeze.14) | copy-start | bytes 6291460
  198.6 38.6 %copy-start.35 = (f32[1,512]{1,0:T(1,128)S(1)}, f32[1,512]{1,0:T(1,128)}, u32[]{:S(2)}) copy-start(f32[1,512]{1,0:T(1,128)} %get-tuple-element.52) | copy-start | bytes 6148
  237.2 6.4 copy-start.9
  237.2 12.3 %slice-start = ((s8[10485760]{0:T(1024)(128)(4,1)}), s8[4194304]{0:T(1024)(128)(4,1)S(1)}, s32[]{:S(2)}) async-start(s8[10485760]{0:T(1024)(128)(4,1)} %bitcast.159), calls=%async_computation.12 | async-start | bytes 8388608
  243.6 5.9 slice-start.1
  243.6 5.9 slice-start.2
  252.7 45.3 %copy-start.15 = (f32[1,1,5120]{2,0,1:T(1,128)S(1)}, f32[1,1,5120]{2,0,1:T(1,128)}, u32[]{:S(2)}) copy-start(f32[1,1,5120]{2,0,1:T(1,128)} %get-tuple-element.23) | copy-start | bytes 61444
  252.7 45.3 %copy-start.16 = (f32[1,1,5120]{2,0,1:T(1,128)S(1)}, f32[1,1,5120]{2,0,1:T(1,128)}, u32[]{:S(2)}) copy-start(f32[1,1,5120]{2,0,1:T(1,128)} %get-tuple-element.24) | copy-start | bytes 61444
  252.7 45.4 %copy-start.17 = (f32[1,1,5120]{2,0,1:T(1,128)S(1)}, f32[1,1,5120]{2,0,1:T(1,128)}, u32[]{:S(2)}) copy-start(f32[1,1,5120]{2,0,1:T(1,128)} %get-tuple-element.25) | copy-start | bytes 61444
  252.7 45.4 %copy-start.18 = (f32[1,1,5120]{2,0,1:T(1,128)S(1)}, f32[1,1,5120]{2,0,1:T(1,128)}, u32[]{:S(2)}) copy-start(f32[1,1,5120]{2,0,1:T(1,128)} %get-tuple-element.26) | copy-start | bytes 61444
  252.8 45.4 %copy-start.19 = (f32[1,1,5120]{2,0,1:T(1,128)S(1)}, f32[1,1,5120]{2,0,1:T(1,128)}, u32[]{:S(2)}) copy-start(f32[1,1,5120]{2,0,1:T(1,128)} %get-tuple-element.27) | copy-start | bytes 61444
  252.8 45.4 %copy-start.20 = (f32[1,1,5120]{2,0,1:T(1,128)S(1)}, f32[1,1,5120]{2,0,1:T(1,128)}, u32[]{:S(2)}) copy-start(f32[1,1,5120]{2,0,1:T(1,128)} %get-tuple-element.28) | copy-start | bytes 61444
  252.8 185.8 %all-gather.12.cloned.1.call-start = ((), (), s32[]{:S(2)}) async-start(), calls=%async_computation.9 | async-start | bytes 13107200 | tf_op jit(solution)/shard_map/all_gather | solution.py:120
  253.4 368.7 %all-gather.14.cloned.1.call-start = ((), (), s32[]{:S(2)}) async-start(), calls=%async_computation.10 | async-start | bytes 13107200 | tf_op jit(solution)/shard_map/all_gather | solution.py:121
  254.0 398.6 %all-gather.10.cloned.1.call-start = ((), (), s32[]{:S(2)}) async-start(), calls=%async_computation.8 | async-start | bytes 2949120 | tf_op jit(solution)/shard_map/all_gather | solution.py:106
  299.3 368.4 %copy-start.37 = (s32[1,16]{1,0:T(1,128)S(1)}, s32[1,16]{1,0:T(1,128)}, u32[]{:S(2)}) copy-start(s32[1,16]{1,0:T(1,128)} %param.26) | copy-start | bytes 196
  299.3 368.4 %copy-start.8 = (bf16[256,4,128]{2,0,1:T(8,128)(2,1)S(1)}, bf16[256,4,128]{2,0,1:T(8,128)(2,1)}, u32[]{:S(2)}) copy-start(bf16[256,4,128]{2,0,1:T(8,128)(2,1)} %copy-done.7) | copy-start | bytes 786436
  299.3 368.8 %copy-start.6 = (bf16[256,512]{1,0:T(8,128)(2,1)S(1)}, bf16[256,512]{1,0:T(8,128)(2,1)}, u32[]{:S(2)}) copy-start(bf16[256,512]{1,0:T(8,128)(2,1)} %copy-done.5) | copy-start | bytes 786436
  299.3 412.2 %reduce-scatter.8.cloned.1.call-start = ((), (), s32[]{:S(2)}) async-start(), calls=%async_computation.11 | async-start | bytes 2949120 | tf_op jit(solution)/shard_map/reduce_scatter | solution.py:109
  652.5 61.0 %copy-start.1 = (bf16[4,5120,32]{1,2,0:T(8,128)(2,1)S(1)}, bf16[4,5120,32]{1,2,0:T(8,128)(2,1)}, u32[]{:S(2)}) copy-start(bf16[4,5120,32]{1,2,0:T(8,128)(2,1)} %param.21) | copy-start | bytes 3932164
  667.7 43.8 %copy-start.21 = (f32[1,1,5120]{2,0,1:T(1,128)S(1)}, f32[1,1,5120]{2,0,1:T(1,128)}, u32[]{:S(2)}) copy-start(f32[1,1,5120]{2,0,1:T(1,128)} %get-tuple-element.22) | copy-start | bytes 61444
  667.7 43.8 %copy-start.22 = (f32[1,1,5120]{2,0,1:T(1,128)S(1)}, f32[1,1,5120]{2,0,1:T(1,128)}, u32[]{:S(2)}) copy-start(f32[1,1,5120]{2,0,1:T(1,128)} %get-tuple-element.29) | copy-start | bytes 61444
  667.7 43.8 %copy-start.23 = (f32[1,1,5120]{2,0,1:T(1,128)S(1)}, f32[1,1,5120]{2,0,1:T(1,128)}, u32[]{:S(2)}) copy-start(f32[1,1,5120]{2,0,1:T(1,128)} %get-tuple-element.30) | copy-start | bytes 61444
  667.7 43.9 %copy-start.24 = (f32[1,1,5120]{2,0,1:T(1,128)S(1)}, f32[1,1,5120]{2,0,1:T(1,128)}, u32[]{:S(2)}) copy-start(f32[1,1,5120]{2,0,1:T(1,128)} %get-tuple-element.31) | copy-start | bytes 61444
  669.5 44.0 %copy-start.11 = (bf16[2,16,16,512]{3,2,1,0:T(8,128)(2,1)}, bf16[2,16,16,512]{3,2,1,0:T(8,128)(2,1)S(1)}, u32[]{:S(2)}) copy-start(bf16[2,16,16,512]{3,2,1,0:T(8,128)(2,1)S(1)} %scatter_fusion) | copy-start | bytes 1572868
  (2 other events, 3.6 us)
Sparse Core Ops, SparseCore 0:
  16.3 33.5 all-gather.5
  141.8 43.6 reduce-scatter.3
  188.2 30.0 all-gather.7
  252.9 43.6 reduce-scatter.5
  667.8 43.6 reduce-scatter.7
Sparse Core Ops, SparseCore 1:
  254.8 183.7 all-gather.11
  440.1 181.9 all-gather.13
  624.4 28.1 all-gather.9
where the time goes:
time: 723 us; the launch traced here: 721 us
  waiting for transfers between devices  509 us (70%)
  local copies, waits for them, and re-layouts  61.7 us (9%)
  matrix products  60.8 us (8%)
  blocking collectives  47.6 us (7%)
  other arithmetic  19.5 us (3%)
  between operations  16.2 us (2%)
    all_gather x1, waiting for transfers between devices, body(): lax.all_gather(feedforward_down, 'req', axis=1, tiled=True)  183 us
    all_gather x1, waiting for transfers between devices, body(): lax.all_gather(feedforward_up, 'req', axis=0, tiled=True)  139 us
    reduce_scatter x3, waiting for transfers between devices, sum_rows(): lax.psum_scatter(term_fn(jnp.int32(0), own_count * lax.axis_size('mlp'))....  127 us
    all_gather x3, waiting for transfers between devices, over_group(): lax.all_gather(own_rows, 'mlp', axis=0, tiled=True)  50.2 us
    psum x3, blocking collectives, global_sum(): lax.psum(as_sent(pieces), 'mlp')  47.6 us
    unnamed x85, local copies, waits for them, and re-layouts  30 us
    dot_general x1, matrix products, down_term(): return jnp.dot(hidden, down_full, preferred_element_type=jnp.float32)  15.1 us
  transfers between devices with their start and end apart: 9, of which 8 were waited for; matrix products, arithmetic and copies ran while one was open for 9% of the time, Pallas kernels for 0%

commit v1 on v0

--- a/solution.py
+++ b/solution.py
@@ -7,6 +7,18 @@
 HD = 128
 PAGE = 16
 EPSILON = 1e-06
+
+
+def expand_the_classes(v0, dim_i, block_in):
+    inter = v0.shape
+    parts_out = v0.reshape(*inter[:dim_i], block_in, inter[dim_i] // block_in, *inter[dim_i + 1 :])
+    return jnp.moveaxis(parts_out, dim_i, 0)
+
+
+def _recover_sector(local_block, ndim_at):
+    found_now = list(local_block.shape[1:])
+    found_now[ndim_at] *= local_block.shape[0]
+    return jnp.moveaxis(local_block, 0, ndim_at).reshape(found_now)
 
 
 def as_sent(array):
@@ -120,9 +132,16 @@
         lax.all_gather(feedforward_up, "req", axis=0, tiled=True),
         lax.all_gather(feedforward_down, "req", axis=1, tiled=True),
     )
-    adapter_up_weight = lax.all_to_all(
-        adapter_up_maps, "mlp", split_axis=3, concat_axis=0, tiled=True
-    )
+    local_next = lax.axis_size("mlp")
+    a_next = lax.axis_index("mlp")
+    then, h_now = (local_next, a_next)
+    lower = expand_the_classes(adapter_up_maps, 3, then)
+    store = [lower[h_now]]
+    for s in range(1, then):
+        extra = lower[h_now ^ s]
+        store.append(lax.ppermute(extra, "mlp", [(dev_j, dev_j ^ s) for dev_j in range(then)]))
+    lower = jnp.stack(store, axis=0)[h_now ^ jnp.arange(then)]
+    adapter_up_weight = _recover_sector(lower, 0)
     slot_total = adapter_up_weight.shape[0]
     bounds = jnp.cumsum(lengths[0])
     position = jnp.arange(group_rows, dtype=jnp.int32)

time: 723 us -> 701 us (0.970)
  local copies, waits for them, and re-layouts: 61.7 us -> 35.2 us
    unnamed x85 -> x103, local copies, waits for them, and re-layouts: 30 us -> 10.6 us
    all_to_all x1 -> x0, local copies, waits for them, and re-layouts: 10.8 us -> none  [body(): lax.all_to_all(adapter_up_maps, 'mlp', split_axis=3, concat_axis=0, tiled...]
    all_to_all x1 -> x0, waiting for transfers between devices: 8.27 us -> none  [body(): lax.all_to_all(adapter_up_maps, 'mlp', split_axis=3, concat_axis=0, tiled...]
    ppermute x0 -> x7, starting transfers between devices: none -> 7.8 us  [body(): lax.ppermute(extra, 'mlp', [(dev_j, dev_j ^ s) for dev_j in range(then)])]
    ppermute x0 -> x7, waiting for transfers between devices: none -> 7.36 us  [body(): lax.ppermute(extra, 'mlp', [(dev_j, dev_j ^ s) for dev_j in range(then)])]
  transfers between devices with their start and end apart: 9 -> 15, of which waited for: 8 -> 10; matrix products, arithmetic and copies ran while one was open for 9% -> 5% of each run, Pallas kernels for 0% -> 0%
where the time goes in v1:
time: 701 us; the launch traced here: 700 us
  waiting for transfers between devices  511 us (73%)
  matrix products  59.8 us (9%)
  blocking collectives  49.9 us (7%)
  local copies, waits for them, and re-layouts  35.2 us (5%)
  other arithmetic  19.3 us (3%)
  between operations  16.4 us (2%)
  starting transfers between devices  8.39 us (1%)
    all_gather x1, waiting for transfers between devices, body(): lax.all_gather(feedforward_down, 'req', axis=1, tiled=True)  183 us
    all_gather x1, waiting for transfers between devices, body(): lax.all_gather(feedforward_up, 'req', axis=0, tiled=True)  139 us
    reduce_scatter x3, waiting for transfers between devices, sum_rows(): lax.psum_scatter(term_fn(jnp.int32(0), own_count * lax.axis_size('mlp'))....  127 us
    all_gather x3, waiting for transfers between devices, over_group(): lax.all_gather(own_rows, 'mlp', axis=0, tiled=True)  53.3 us
    psum x3, blocking collectives, global_sum(): lax.psum(as_sent(pieces), 'mlp')  49.9 us
    dot_general x1, matrix products, down_term(): return jnp.dot(hidden, down_full, preferred_element_type=jnp.float32)  15 us
  transfers between devices with their start and end apart: 15, of which 10 were waited for; matrix products, arithmetic and copies ran while one was open for 5% of the time, Pallas kernels for 0%

profile of v1, /device:TPU:0, one launch (start us, length us, event | category | flops | bytes accessed | tf_op | source)
XLA Modules:
  0.0 699.7 jit_solution(7017948126107459432)
XLA Ops:
  8.1 0.9 reduce-window.8
  9.2 2.7 fusion.94
  11.8 1.1 convert_reduce_fusion.2
  13.0 1.2 fusion.48
  14.2 2.1 fusion.51
  16.5 1.6 copy.84
  18.1 3.1 constant_dynamic-slice_fusion
  22.3 2.6 collective-permute-start.1
  25.1 1.9 collective-permute-start.3
  29.1 2.4 compare_select_fusion.11
  33.8 1.0 bitcast_dynamic-update-slice_fusion
  34.8 1.6 copy.116
  38.6 2.5 collective-permute-start.5
  43.1 0.9 bitcast_dynamic-update-slice_fusion.5
  44.0 0.9 bitcast_dynamic-update-slice_fusion.4
  45.0 0.9 bitcast_dynamic-update-slice_fusion.3
  45.9 1.8 collective-permute-done.5
  47.7 5.5 collective-permute-done.6
  54.1 3.0 all-gather.6.cloned.1.call-done
  57.1 2.7 fusion.100
  59.9 24.6 %psum.28 = bf16[256,32]{0,1:T(8,128)(2,1)S(1)} all-reduce(bf16[256,32]{0,1:T(8,128)(2,1)S(1)} %multiply_reduce_fusion.3), channel_id=1, replica_groups=mesh['req'=4,'mlp'=8] {'mlp'}, use_global_device_ids=true, to_apply=%region_5.6 | all-reduce | flops 8192 | bytes 32768 | tf_op jit(solution)/shard_map/psum | solution.py:129
  85.3 4.9 fusion.7
  90.7 4.1 multiply_reduce_fusion.1
  94.8 12.0 %all-reduce = (bf16[256]{0:T(256)(128)(2,1)S(1)}, bf16[256]{0:T(256)(128)(2,1)S(1)}) all-reduce(bf16[256]{0:T(256)(128)(2,1)S(1)} %get-tuple-element.70, bf16[256]{0:T(256)(128)(2,1)S(1)} %get-tuple-element.72), channel_id=1, replica_groups=mesh['req'=4,'mlp'=8] {'mlp'}, use_global_device_ids=true, to_apply=%region_9.10 | all-reduce | flops 512 | bytes 2048 | tf_op jit(solution)/shard_map/psum | solution.py:129
  108.1 4.8 fusion.9
  115.7 5.6 convolution_convert_fusion.2
  121.3 1.2 fusion.95
  122.5 41.9 %reduce-scatter.4.cloned.1.call-done = bf16[32,5120]{1,0:T(8,128)(2,1)} async-done(((bf16[256,5120]{1,0:T(8,128)(2,1)}), bf16[32,5120]{1,0:T(8,128)(2,1)}) %reduce-scatter.4.cloned.1.call-update) | async-done | bytes 327696 | tf_op jit(solution)/shard_map/reduce_scatter | solution.py:121
  164.4 1.4 convert_reduce_fusion.1
  167.0 4.0 fusion.90
  171.0 4.0 reshape_squeeze.14
  174.9 2.1 reshape.485
  177.4 19.8 %all-gather.8.cloned.1.call-done = bf16[256,5120]{1,0:T(8,128)(2,1)} async-done(((bf16[32,5120]{1,0:T(8,128)(2,1)}), bf16[256,5120]{1,0:T(8,128)(2,1)}) %all-gather.8.cloned.1.call-update) | async-done | bytes 2621456 | tf_op jit(solution)/shard_map/all_gather | solution.py:118
  197.2 5.6 multiply_reduce_fusion
  202.8 13.3 %psum.31 = bf16[256]{0:T(256)(128)(2,1)S(1)} all-reduce(bf16[256]{0:T(256)(128)(2,1)S(1)} %get-tuple-element.74), channel_id=1, replica_groups=mesh['req'=4,'mlp'=8] {'mlp'}, use_global_device_ids=true, to_apply=%region_15.16 | all-reduce | flops 256 | bytes 1024 | tf_op jit(solution)/shard_map/psum | solution.py:129
  216.2 6.5 fusion
  222.6 5.9 fusion.24
  228.6 3.1 convolution_convert_fusion.1
  233.0 42.6 %reduce-scatter.6.cloned.1.call-done = bf16[32,5120]{1,0:T(8,128)(2,1)} async-done(((bf16[256,5120]{1,0:T(8,128)(2,1)}), bf16[32,5120]{1,0:T(8,128)(2,1)}) %reduce-scatter.6.cloned.1.call-update) | async-done | bytes 327696 | tf_op jit(solution)/shard_map/reduce_scatter | solution.py:121
  275.6 1.2 convert_reduce_fusion
  277.1 1.1 fusion.44
  278.6 139.0 %all-gather.12.cloned.1.call-done = bf16[5120,1024]{1,0:T(8,128)(2,1)} async-done(((bf16[1280,1024]{1,0:T(8,128)(2,1)}), bf16[5120,1024]{1,0:T(8,128)(2,1)}) %all-gather.12.cloned.1.call-update) | async-done | bytes 10485776 | tf_op jit(solution)/shard_map/all_gather | solution.py:132
  417.6 183.4 %all-gather.14.cloned.1.call-done = bf16[1024,5120]{1,0:T(8,128)(2,1)} async-done(((bf16[1024,1280]{1,0:T(8,128)(2,1)}), bf16[1024,5120]{1,0:T(8,128)(2,1)}) %all-gather.14.cloned.1.call-update) | async-done | bytes 10485776 | tf_op jit(solution)/shard_map/all_gather | solution.py:133
  601.0 30.5 %all-gather.10.cloned.1.call-done = bf16[256,5120]{1,0:T(8,128)(2,1)} async-done(((bf16[32,5120]{1,0:T(8,128)(2,1)}), bf16[256,5120]{1,0:T(8,128)(2,1)}) %all-gather.10.cloned.1.call-update) | async-done | bytes 2621456 | tf_op jit(solution)/shard_map/all_gather | solution.py:118
  631.5 15.0 %convolution_convert_fusion = bf16[256,5120]{1,0:T(8,128)(2,1)} fusion(bf16[1024,5120]{1,0:T(8,128)(2,1)} %all-gather.14.cloned.1.call-done, bf16[256,5120]{1,0:T(8,128)(2,1)} %all-gather.10.cloned.1.call-done, bf16[5120,1024]{1,0:T(8,128)(2,1)} %all-gather.12.cloned.1.call-done), kind=kOutput, calls=%fused_computation.7 | convolution fusion | flops 5372379136 | bytes 26214400 | tf_op jit(solution)/shard_map/dot_general | solution.py:273
  647.1 1.2 scatter_fusion
  648.4 42.1 %reduce-scatter.8.cloned.1.call-done = bf16[32,5120]{1,0:T(8,128)(2,1)} async-done(((bf16[256,5120]{1,0:T(8,128)(2,1)}), bf16[32,5120]{1,0:T(8,128)(2,1)}) %reduce-scatter.8.cloned.1.call-update) | async-done | bytes 327696 | tf_op jit(solution)/shard_map/reduce_scatter | solution.py:121
  690.4 2.0 fusion.54
  (184 shorter events, 20.2 us)
Async XLA Ops:
  8.0 49.1 %copy-start = (bf16[4,5120,32]{1,2,0:T(8,128)(2,1)S(1)}, bf16[4,5120,32]{1,2,0:T(8,128)(2,1)}, u32[]{:S(2)}) copy-start(bf16[4,5120,32]{1,2,0:T(8,128)(2,1)} %param.21) | copy-start | bytes 3932164
  8.0 49.1 %all-gather.6.cloned.1.call-start = ((), (), s32[]{:S(2)}) async-start(), calls=%async_computation.3 | async-start | bytes 2949120 | tf_op jit(solution)/shard_map/all_gather | solution.py:118
  9.2 12.0 %copy-start.30 = (pred[32]{0:T(512)(128)(4,1)}, pred[32]{0:T(512)(128)(4,1)S(1)}, u32[]{:S(2)}) copy-start(pred[32]{0:T(512)(128)(4,1)S(1)} %get-tuple-element.68) | copy-start | bytes 100
  16.3 10.7 %copy-start.37 = (s32[3,256]{1,0:T(4,128)S(1)}, s32[3,256]{1,0:T(4,128)}, u32[]{:S(2)}) copy-start(s32[3,256]{1,0:T(4,128)} %param.25) | copy-start | bytes 9220
  16.4 10.8 %copy-start.39 = (s32[4]{0:T(128)S(1)}, s32[4]{0:T(128)}, u32[]{:S(2)}) copy-start(s32[4]{0:T(128)} %param.19) | copy-start | bytes 52
  16.4 10.8 %copy-start.2 = (s32[32]{0:T(128)S(1)}, s32[32]{0:T(128)}, u32[]{:S(2)}) copy-start(s32[32]{0:T(128)} %param.20) | copy-start | bytes 388
  16.4 148.0 %reduce-scatter.4.cloned.1.call-start = ((), (), s32[]{:S(2)}) async-start(), calls=%async_computation.4 | async-start | bytes 2949120 | tf_op jit(solution)/shard_map/reduce_scatter | solution.py:121
  18.1 13.5 %copy-start.36 = (f32[3,512]{1,0:T(4,128)S(1)}, f32[3,512]{1,0:T(4,128)}, u32[]{:S(2)}) copy-start(f32[3,512]{1,0:T(4,128)} %param.24) | copy-start | bytes 18436
  21.2 15.3 %copy-start.13 = (bf16[4,2,16,1,512]{4,3,2,1,0:T(2,128)(2,1)S(1)}, bf16[4,2,16,1,512]{4,3,2,1,0:T(2,128)(2,1)}, u32[]{:S(2)}) copy-start(bf16[4,2,16,1,512]{4,3,2,1,0:T(2,128)(2,1)} %get-tuple-element.18) | copy-start | bytes 393220
  21.9 16.7 %collective-permute-start = (bf16[4,2,16,512]{3,2,1,0:T(8,128)(2,1)}, bf16[4,2,16,512]{3,2,1,0:T(8,128)(2,1)}, u32[]{:S(2)}, u32[]{:S(2)}) collective-permute-start(bf16[4,2,16,512]{3,2,1,0:T(8,128)(2,1)} %bitcast.158), channel_id=1, source_target_pairs={{0,1},{1,0},{2,3},{3,2},{4,5},{5,4},{6,7},{7,6},{8,9},{9,8},{10,11... | collective-permute-start | bytes 393224 | tf_op jit(solution)/shard_map/ppermute | solution.py:142
  22.3 19.6 %collective-permute-start.1 = (bf16[4,2,16,512]{3,2,1,0:T(8,128)(2,1)S(1)}, bf16[4,2,16,512]{3,2,1,0:T(8,128)(2,1)}, u32[]{:S(2)}, u32[]{:S(2)}) collective-permute-start(bf16[4,2,16,512]{3,2,1,0:T(8,128)(2,1)S(1)} %bitcast.173), channel_id=1, source_target_pairs={{0,2},{1,3},{2,0},{3,1},{4,6},{5,7},{6,4},{7,5},{8,10},{9,11},{10,... | collective-permute-start | bytes 393224 | tf_op jit(solution)/shard_map/ppermute | solution.py:142
  24.9 18.2 %collective-permute-start.2 = (bf16[4,2,16,512]{3,2,1,0:T(8,128)(2,1)S(1)}, bf16[4,2,16,512]{3,2,1,0:T(8,128)(2,1)}, u32[]{:S(2)}, u32[]{:S(2)}) collective-permute-start(bf16[4,2,16,512]{3,2,1,0:T(8,128)(2,1)S(1)} %bitcast.172), channel_id=1, source_target_pairs={{0,3},{1,2},{2,1},{3,0},{4,7},{5,6},{6,5},{7,4},{8,11},{9,10},{10,... | collective-permute-start | bytes 393224 | tf_op jit(solution)/shard_map/ppermute | solution.py:142
  25.1 18.9 %collective-permute-start.3 = (bf16[4,2,16,512]{3,2,1,0:T(8,128)(2,1)S(1)}, bf16[4,2,16,512]{3,2,1,0:T(8,128)(2,1)}, u32[]{:S(2)}, u32[]{:S(2)}) collective-permute-start(bf16[4,2,16,512]{3,2,1,0:T(8,128)(2,1)S(1)} %bitcast.171), channel_id=1, source_target_pairs={{0,4},{1,5},{2,6},{3,7},{4,0},{5,1},{6,2},{7,3},{8,12},{9,13},{10,... | collective-permute-start | bytes 393224 | tf_op jit(solution)/shard_map/ppermute | solution.py:142
  27.0 17.9 %collective-permute-start.4 = (bf16[4,2,16,512]{3,2,1,0:T(8,128)(2,1)S(1)}, bf16[4,2,16,512]{3,2,1,0:T(8,128)(2,1)}, u32[]{:S(2)}, u32[]{:S(2)}) collective-permute-start(bf16[4,2,16,512]{3,2,1,0:T(8,128)(2,1)S(1)} %bitcast.170), channel_id=1, source_target_pairs={{0,5},{1,4},{2,7},{3,6},{4,1},{5,0},{6,3},{7,2},{8,13},{9,12},{10,... | collective-permute-start | bytes 393224 | tf_op jit(solution)/shard_map/ppermute | solution.py:142
  38.6 9.1 %collective-permute-start.5 = (bf16[4,2,16,512]{3,2,1,0:T(8,128)(2,1)}, bf16[4,2,16,512]{3,2,1,0:T(8,128)(2,1)S(1)}, u32[]{:S(2)}, u32[]{:S(2)}) collective-permute-start(bf16[4,2,16,512]{3,2,1,0:T(8,128)(2,1)} %bitcast.175), channel_id=1, source_target_pairs={{0,6},{1,7},{2,4},{3,5},{4,2},{5,3},{6,0},{7,1},{8,14},{9,15},{10,... | collective-permute-start | bytes 393224 | tf_op jit(solution)/shard_map/ppermute | solution.py:142
  42.0 11.2 %collective-permute-start.6 = (bf16[4,2,16,512]{3,2,1,0:T(8,128)(2,1)}, bf16[4,2,16,512]{3,2,1,0:T(8,128)(2,1)S(1)}, u32[]{:S(2)}, u32[]{:S(2)}) collective-permute-start(bf16[4,2,16,512]{3,2,1,0:T(8,128)(2,1)} %bitcast.174), channel_id=1, source_target_pairs={{0,7},{1,6},{2,5},{3,4},{4,3},{5,2},{6,1},{7,0},{8,15},{9,14},{10,... | collective-permute-start | bytes 393224 | tf_op jit(solution)/shard_map/ppermute | solution.py:142
  54.1 30.4 %copy-start.17 = (f32[256,32]{0,1:T(8,128)S(1)}, f32[256,32]{0,1:T(8,128)}, u32[]{:S(2)}) copy-start(f32[256,32]{0,1:T(8,128)} %fusion.67) | copy-start | bytes 98308
  90.6 16.2 %copy-start.35 = (f32[1,512]{1,0:T(1,128)S(1)}, f32[1,512]{1,0:T(1,128)}, u32[]{:S(2)}) copy-start(f32[1,512]{1,0:T(1,128)} %get-tuple-element.62) | copy-start | bytes 6148
  94.8 12.7 %copy-start.34 = (f32[1,512]{1,0:T(1,128)S(1)}, f32[1,512]{1,0:T(1,128)}, u32[]{:S(2)}) copy-start(f32[1,512]{1,0:T(1,128)} %get-tuple-element.61) | copy-start | bytes 6148
  115.6 48.7 %copy-start.3 = (bf16[32,5120]{1,0:T(8,128)(2,1)S(1)}, bf16[32,5120]{1,0:T(8,128)(2,1)}, u32[]{:S(2)}) copy-start(bf16[32,5120]{1,0:T(8,128)(2,1)} %param.16) | copy-start | bytes 983044
  115.6 48.7 %copy-start.28 = (f32[1,1,5120]{2,0,1:T(1,128)S(1)}, f32[1,1,5120]{2,0,1:T(1,128)}, u32[]{:S(2)}) copy-start(f32[1,1,5120]{2,0,1:T(1,128)} %get-tuple-element.48) | copy-start | bytes 61444
  115.6 48.7 %copy-start.31 = (pred[32]{0:T(512)(128)(4,1)S(1)}, pred[32]{0:T(512)(128)(4,1)}, u32[]{:S(2)}) copy-start(pred[32]{0:T(512)(128)(4,1)} %copy-done.30) | copy-start | bytes 100
  115.7 48.7 %copy-start.33 = (pred[32]{0:T(512)(128)(4,1)S(1)}, pred[32]{0:T(512)(128)(4,1)}, u32[]{:S(2)}) copy-start(pred[32]{0:T(512)(128)(4,1)} %copy-done.32) | copy-start | bytes 100
  121.2 44.8 %copy-start.29 = (f32[5120]{0:T(1024)S(1)}, f32[5120]{0:T(1024)}, u32[]{:S(2)}) copy-start(f32[5120]{0:T(1024)} %param.28) | copy-start | bytes 61444
  121.3 75.9 %all-gather.8.cloned.1.call-start = ((), (), s32[]{:S(2)}) async-start(), calls=%async_computation.5 | async-start | bytes 2949120 | tf_op jit(solution)/shard_map/all_gather | solution.py:118
  166.9 108.7 %reduce-scatter.6.cloned.1.call-start = ((), (), s32[]{:S(2)}) async-start(), calls=%async_computation.6 | async-start | bytes 2949120 | tf_op jit(solution)/shard_map/reduce_scatter | solution.py:121
  177.4 38.7 %copy-start.10 = (bf16[2048,4,128]{2,1,0:T(4,128)(2,1)S(1)}, bf16[2048,4,128]{2,1,0:T(4,128)(2,1)}, u32[]{:S(2)}) copy-start(bf16[2048,4,128]{2,1,0:T(4,128)(2,1)} %reshape_squeeze.14) | copy-start | bytes 6291460
  177.4 38.7 %copy-start.38 = (f32[1,512]{1,0:T(1,128)S(1)}, f32[1,512]{1,0:T(1,128)}, u32[]{:S(2)}) copy-start(f32[1,512]{1,0:T(1,128)} %get-tuple-element.60) | copy-start | bytes 6148
  216.1 12.4 %slice-start = ((s8[10485760]{0:T(1024)(128)(4,1)}), s8[4194304]{0:T(1024)(128)(4,1)S(1)}, s32[]{:S(2)}) async-start(s8[10485760]{0:T(1024)(128)(4,1)} %bitcast.203), calls=%async_computation.11 | async-start | bytes 8388608
  231.7 45.3 %copy-start.18 = (f32[1,1,5120]{2,0,1:T(1,128)S(1)}, f32[1,1,5120]{2,0,1:T(1,128)}, u32[]{:S(2)}) copy-start(f32[1,1,5120]{2,0,1:T(1,128)} %get-tuple-element.31) | copy-start | bytes 61444
  231.7 45.3 %copy-start.19 = (f32[1,1,5120]{2,0,1:T(1,128)S(1)}, f32[1,1,5120]{2,0,1:T(1,128)}, u32[]{:S(2)}) copy-start(f32[1,1,5120]{2,0,1:T(1,128)} %get-tuple-element.32) | copy-start | bytes 61444
  231.7 45.4 %copy-start.20 = (f32[1,1,5120]{2,0,1:T(1,128)S(1)}, f32[1,1,5120]{2,0,1:T(1,128)}, u32[]{:S(2)}) copy-start(f32[1,1,5120]{2,0,1:T(1,128)} %get-tuple-element.33) | copy-start | bytes 61444
  231.7 45.4 %copy-start.21 = (f32[1,1,5120]{2,0,1:T(1,128)S(1)}, f32[1,1,5120]{2,0,1:T(1,128)}, u32[]{:S(2)}) copy-start(f32[1,1,5120]{2,0,1:T(1,128)} %get-tuple-element.34) | copy-start | bytes 61444
  231.7 45.4 %copy-start.22 = (f32[1,1,5120]{2,0,1:T(1,128)S(1)}, f32[1,1,5120]{2,0,1:T(1,128)}, u32[]{:S(2)}) copy-start(f32[1,1,5120]{2,0,1:T(1,128)} %get-tuple-element.35) | copy-start | bytes 61444
  231.8 45.4 %copy-start.23 = (f32[1,1,5120]{2,0,1:T(1,128)S(1)}, f32[1,1,5120]{2,0,1:T(1,128)}, u32[]{:S(2)}) copy-start(f32[1,1,5120]{2,0,1:T(1,128)} %get-tuple-element.36) | copy-start | bytes 61444
  231.8 185.8 %all-gather.12.cloned.1.call-start = ((), (), s32[]{:S(2)}) async-start(), calls=%async_computation.8 | async-start | bytes 13107200 | tf_op jit(solution)/shard_map/all_gather | solution.py:132
  232.4 368.7 %all-gather.14.cloned.1.call-start = ((), (), s32[]{:S(2)}) async-start(), calls=%async_computation.9 | async-start | bytes 13107200 | tf_op jit(solution)/shard_map/all_gather | solution.py:133
  233.0 398.6 %all-gather.10.cloned.1.call-start = ((), (), s32[]{:S(2)}) async-start(), calls=%async_computation.7 | async-start | bytes 2949120 | tf_op jit(solution)/shard_map/all_gather | solution.py:118
  278.3 368.3 %copy-start.40 = (s32[1,16]{1,0:T(1,128)S(1)}, s32[1,16]{1,0:T(1,128)}, u32[]{:S(2)}) copy-start(s32[1,16]{1,0:T(1,128)} %param.26) | copy-start | bytes 196
  278.3 368.3 %copy-start.8 = (bf16[256,4,128]{2,0,1:T(8,128)(2,1)S(1)}, bf16[256,4,128]{2,0,1:T(8,128)(2,1)}, u32[]{:S(2)}) copy-start(bf16[256,4,128]{2,0,1:T(8,128)(2,1)} %copy-done.7) | copy-start | bytes 786436
  278.3 368.7 %copy-start.6 = (bf16[256,512]{1,0:T(8,128)(2,1)S(1)}, bf16[256,512]{1,0:T(8,128)(2,1)}, u32[]{:S(2)}) copy-start(bf16[256,512]{1,0:T(8,128)(2,1)} %copy-done.5) | copy-start | bytes 786436
  278.3 412.1 %reduce-scatter.8.cloned.1.call-start = ((), (), s32[]{:S(2)}) async-start(), calls=%async_computation.10 | async-start | bytes 2949120 | tf_op jit(solution)/shard_map/reduce_scatter | solution.py:121
  646.5 43.9 %copy-start.24 = (f32[1,1,5120]{2,0,1:T(1,128)S(1)}, f32[1,1,5120]{2,0,1:T(1,128)}, u32[]{:S(2)}) copy-start(f32[1,1,5120]{2,0,1:T(1,128)} %get-tuple-element.30) | copy-start | bytes 61444
  646.5 43.9 %copy-start.25 = (f32[1,1,5120]{2,0,1:T(1,128)S(1)}, f32[1,1,5120]{2,0,1:T(1,128)}, u32[]{:S(2)}) copy-start(f32[1,1,5120]{2,0,1:T(1,128)} %get-tuple-element.37) | copy-start | bytes 61444
  646.5 43.9 %copy-start.26 = (f32[1,1,5120]{2,0,1:T(1,128)S(1)}, f32[1,1,5120]{2,0,1:T(1,128)}, u32[]{:S(2)}) copy-start(f32[1,1,5120]{2,0,1:T(1,128)} %get-tuple-element.38) | copy-start | bytes 61444
  646.5 43.9 %copy-start.27 = (f32[1,1,5120]{2,0,1:T(1,128)S(1)}, f32[1,1,5120]{2,0,1:T(1,128)}, u32[]{:S(2)}) copy-start(f32[1,1,5120]{2,0,1:T(1,128)} %get-tuple-element.39) | copy-start | bytes 61444
  646.5 45.9 %copy-start.1 = (bf16[4,5120,32]{1,2,0:T(8,128)(2,1)S(1)}, bf16[4,5120,32]{1,2,0:T(8,128)(2,1)}, u32[]{:S(2)}) copy-start(bf16[4,5120,32]{1,2,0:T(8,128)(2,1)} %param.21) | copy-start | bytes 3932164
  648.3 44.1 %copy-start.11 = (bf16[2,16,16,512]{3,2,1,0:T(8,128)(2,1)}, bf16[2,16,16,512]{3,2,1,0:T(8,128)(2,1)S(1)}, u32[]{:S(2)}) copy-start(bf16[2,16,16,512]{3,2,1,0:T(8,128)(2,1)S(1)} %scatter_fusion) | copy-start | bytes 1572868
  (11 other events, 45.8 us)
Sparse Core Ops, SparseCore 0:
  16.5 40.5 all-gather.5
  121.4 42.9 reduce-scatter.3
  167.1 30.0 all-gather.7
  231.9 43.6 reduce-scatter.5
  646.7 43.6 reduce-scatter.7
Sparse Core Ops, SparseCore 1:
  233.8 183.7 all-gather.11
  419.1 181.9 all-gather.13
  603.4 28.1 all-gather.9
